TPU v7x, 512 devices: a whole 4x4x16 slice. The times are simulated.
512 devices in a mesh: row: 16 (over y, z_hi), col: 32 (over x, z_lo, core).
Axes of the slice: x: 4, y: 4, z: 16 (z_hi: 4, z_lo: 4; z = z_hi * 4 + z_lo), core: 2. Of those that a mesh axis runs over, the one named last changes fastest.
Arguments:
- inv_known: float32 [8192, 8192], P('row', 'col'), as said below
- pattern: int32 [128, 128], P('row', 'col'), may hold values from 0 to 1, as said below
- factor: float32 [8192, 2, 512], P(('row', 'col')), may hold values from -0.0625 to 0.0625
- listed: int32 [8192, 2], P(('row', 'col')), may hold values 0 or 1
- diag_inverse: float32 [512, 2, 512], P('col'), may hold values from -6 to 6
Outputs:
- inverse_columns: float32 [512, 2, 8192], P('col', None, 'row')
- schur: float32 [512, 2, 512], P('col')
Inputs may be any that keep to these rules, and one draw needn't show every extreme that they name: `inv_known`: symmetric. `pattern`: symmetric; every diagonal tile is present.
All inputs are finite; a program needn't handle non-finite values. No bound on the sum of `listed` on one device may be relied on, other than what follows from the above.
Results may differ from a plain program's by a relative error of at most 0.0001.
Values sent between devices are 32-bit elements; how exact they have to be, the bound alone decides.
A program may use at most 64 MiB of HBM per device.

v0:
```python
import jax
import jax.numpy as jnp
from jax import lax
from jax.sharding import PartitionSpec as P


def in_one_piece(arrays, axis, dim, along):
    columns = [a.reshape(*a.shape[:along], -1) for a in arrays]
    both = jnp.concatenate(columns, axis=along)
    filled, at, finished = (lax.all_gather(both, axis, axis=dim, tiled=True), 0, [])
    for a, column in zip(arrays, columns):
        slab = filled[..., at : at + column.shape[along]]
        finished.append(slab.reshape(*slab.shape[:along], *a.shape[along:]))
        at += column.shape[along]
    return tuple(finished)


def in_blocks(x, dim, peers):
    before, after = (x.shape[:dim], x.shape[dim + 1 :])
    return jnp.moveaxis(x.reshape(*before, peers, -1, *after), dim, 0)


def sum_at_owner(x, axis, dim):
    parts = in_blocks(x, dim, lax.axis_size(axis))
    arrived = lax.all_to_all(parts, axis, split_axis=0, concat_axis=0, tiled=True)
    return arrived.sum(axis=0)


def from_everyone(x, axis):
    copies = jnp.broadcast_to(x, (lax.axis_size(axis), *x.shape))
    return lax.all_to_all(copies, axis, split_axis=0, concat_axis=0, tiled=True)


def of_everyone(x, axis):
    everything = from_everyone(x, axis)
    return jnp.sum(everything, axis=0)


def supernode_pass(present, masked, listed_f, diag_part, ratio):
    row_block, row_listed = in_one_piece((masked, listed_f), "col", 0, 2)
    held = sum_at_owner(
        jnp.einsum("ij,ika->jka", present, row_block, precision=lax.Precision.HIGHEST), "row", 0
    )
    count_row = lax.axis_size("row")
    count_col = lax.axis_size("col")
    local_rows = held.shape[0]
    nodes = held.shape[1]
    narrow = held.shape[2] // count_col
    by_column = lax.all_to_all(held[None], "col", split_axis=3, concat_axis=0, tiled=True)
    grouped = by_column.reshape(count_row, 1, ratio, local_rows, nodes, narrow)
    moved = lax.all_to_all(grouped, "row", split_axis=0, concat_axis=1, tiled=True)
    ordered = jnp.transpose(moved[0], (1, 0, 2, 3, 4)).reshape(
        ratio * count_row * local_rows, nodes, narrow
    )
    summed = jnp.transpose(ordered, (2, 1, 0))
    columns = -summed * jnp.transpose(row_listed)[None, :, :]
    update = jnp.einsum("akj,jkb->akb", columns, row_block, precision=lax.Precision.HIGHEST)
    schur = diag_part - of_everyone(update, "row")
    return (columns, schur)


def local(inv_known, pattern, factor, listed, diag_inverse):
    tile = inv_known.shape[0] // pattern.shape[0]
    flags = pattern.astype(jnp.float32)
    spread = jnp.repeat(jnp.repeat(flags, tile, axis=0), tile, axis=1)
    present = inv_known * spread
    listed_f = listed.astype(jnp.float32)
    masked = factor * listed_f[:, :, None]
    ratio = lax.axis_size("col") // lax.axis_size("row")
    columns, schur = supernode_pass(present, masked, listed_f, diag_inverse, ratio)
    return (columns, schur)


def solution(mesh):
    in_specs = (
        P("row", "col"),
        P("row", "col"),
        P(("row", "col"), None, None),
        P(("row", "col"), None),
        P("col", None, None),
    )
    out_specs = (P("col", None, "row"), P("col", None, None))
    return jax.shard_map(local, mesh=mesh, in_specs=in_specs, out_specs=out_specs, check_vma=False)
```

profile of v0, /device:TPU:32, one launch (start us, length us, event | category | flops | bytes accessed | tf_op | source)
XLA Modules:
  0.0 265.9 jit_solution(16687229242903270589)
XLA Ops:
  7.2 0.7 fusion.8
  8.0 0.9 copy_multiply_fusion
  9.6 1.2 copy.47
  10.8 0.7 convert_element_type.6
  11.7 67.7 %all-gather.2.cloned.1.call-done = f32[512,2,513]{2,0,1:T(8,128)} async-done(((f32[16,2,513]{2,0,1:T(8,128)}), f32[512,2,513]{2,0,1:T(8,128)}) %all-gather.2.cloned.1.call-update) | async-done | bytes 2101264 | tf_op jit(solution)/shard_map/all_gather | solution.py:10
  79.4 3.5 %fusion.2 = f32[256,2,512]{2,0,1:T(8,128)S(1)} fusion(f32[512,2,513]{2,0,1:T(8,128)} %all-gather.2.cloned.1.call-done, f32[512,256]{0,1:T(8,128)S(1)} %bitcast_multiply_fusion), kind=kOutput, calls=%fused_computation.2 | convolution fusion | flops 1610612736 | bytes 3670016 | tf_op jit(solution)/shard_map/ij,ika->jka/dot_general | solution.py:42
  83.0 66.8 %all_to_all.34 = f32[16,16,2,512]{3,1,2,0:T(8,128)S(1)} all-to-all(f32[16,16,2,512]{3,1,2,0:T(8,128)S(1)} %copy.50), channel_id=1, replica_groups=mesh['row'=16,'col'=32] {'row'}, dimensions={0} | all-to-all | bytes 2097152 | tf_op jit(solution)/shard_map/all_to_all | solution.py:25
  150.1 0.7 reshape.37
  150.8 15.7 %all_to_all.35 = f32[32,1,512]{2,1,0:T(1,128)S(1)} all-to-all(f32[32,1,512]{2,1,0:T(1,128)S(1)} %reshape.37), channel_id=1, replica_groups=mesh['row'=16,'col'=32] {'col'}, dimensions={0} | all-to-all | bytes 131072 | tf_op jit(solution)/shard_map/all_to_all | solution.py:49
  167.0 0.8 reduce.2
  167.8 0.7 reshape.38
  168.5 1.2 copy.59
  169.8 1.3 copy.65
  171.1 0.9 reshape.39
  172.0 3.5 %all-to-all-start.2 = ((f32[16,1,1024]{2,1,0:T(1,128)}), f32[16,1,1024]{2,1,0:T(1,128)S(1)}, u32[]{:S(2)}, u32[]{:S(2)}) async-start(f32[16,1,1024]{2,1,0:T(1,128)} %reshape.39), calls=%async_computation.2 | async-start | bytes 131072 | tf_op jit(solution)/shard_map/all_to_all | solution.py:51
  175.7 16.0 %all-to-all-done.2 = f32[16,1,1024]{2,1,0:T(1,128)S(1)} async-done(((f32[16,1,1024]{2,1,0:T(1,128)}), f32[16,1,1024]{2,1,0:T(1,128)S(1)}, u32[]{:S(2)}, u32[]{:S(2)}) %all-to-all-start.2) | async-done | bytes 65568 | tf_op jit(solution)/shard_map/all_to_all | solution.py:51
  191.8 0.8 reduce.3
  192.8 0.8 negate_bitcast_fusion
  193.6 1.5 copy.55
  195.4 1.2 fusion.4
  196.6 1.1 broadcast_in_dim.20
  197.7 3.7 %all-to-all-start.3 = ((f32[16,16,2,512]{3,1,2,0:T(8,128)}), f32[16,16,2,512]{3,1,2,0:T(8,128)S(1)}, u32[]{:S(2)}, u32[]{:S(2)}) async-start(f32[16,16,2,512]{3,1,2,0:T(8,128)} %broadcast_in_dim.20), calls=%async_computation.3 | async-start | bytes 2097152 | tf_op jit(solution)/shard_map/all_to_all | solution.py:31
  201.4 0.7 copy.57
  202.0 56.3 %all-to-all-done.3 = f32[16,16,2,512]{3,1,2,0:T(8,128)S(1)} async-done(((f32[16,16,2,512]{3,1,2,0:T(8,128)}), f32[16,16,2,512]{3,1,2,0:T(8,128)S(1)}, u32[]{:S(2)}, u32[]{:S(2)}) %all-to-all-start.3) | async-done | bytes 1048608 | tf_op jit(solution)/shard_map/all_to_all | solution.py:31
  (22 shorter events, 3.3 us)
Async XLA Ops:
  7.2 72.3 %all-gather.2.cloned.1.call-start = ((), (), s32[]{:S(2)}) async-start(), calls=%async_computation.4 | async-start | bytes 2703360 | tf_op jit(solution)/shard_map/all_gather | solution.py:10
  149.8 25.7 %copy-start = (f32[512,2,513]{2,0,1:T(8,128)S(1)}, f32[512,2,513]{2,0,1:T(8,128)}, u32[]{:S(2)}) copy-start(f32[512,2,513]{2,0,1:T(8,128)} %all-gather.2.cloned.1.call-done) | copy-start | bytes 6303748
  172.0 19.8 %all-to-all-start.2 = ((f32[16,1,1024]{2,1,0:T(1,128)}), f32[16,1,1024]{2,1,0:T(1,128)S(1)}, u32[]{:S(2)}, u32[]{:S(2)}) async-start(f32[16,1,1024]{2,1,0:T(1,128)} %reshape.39), calls=%async_computation.2 | async-start | bytes 131072 | tf_op jit(solution)/shard_map/all_to_all | solution.py:51
  196.6 61.8 %copy-start.1 = (f32[16,2,512]{2,1,0:T(2,128)S(1)}, f32[16,2,512]{2,1,0:T(2,128)}, u32[]{:S(2)}) copy-start(f32[16,2,512]{2,1,0:T(2,128)} %param.9) | copy-start | bytes 196612
  197.7 60.6 %all-to-all-start.3 = ((f32[16,16,2,512]{3,1,2,0:T(8,128)}), f32[16,16,2,512]{3,1,2,0:T(8,128)S(1)}, u32[]{:S(2)}, u32[]{:S(2)}) async-start(f32[16,16,2,512]{3,1,2,0:T(8,128)} %broadcast_in_dim.20), calls=%async_computation.3 | async-start | bytes 2097152 | tf_op jit(solution)/shard_map/all_to_all | solution.py:31
Sparse Core Ops, SparseCore 0:
  10.1 69.3 all-gather.1
where the time goes:
time: 267 us; the launch traced here: 266 us
  waiting for transfers between devices  140 us (52%)
  blocking collectives  82.5 us (31%)
  between operations  14.2 us (5%)
  local copies, waits for them, and re-layouts  11.8 us (4%)
  starting transfers between devices  7.2 us (3%)
  other arithmetic  5.58 us (2%)
  matrix products  4.68 us (2%)
    all_gather x1, waiting for transfers between devices, in_one_piece(): lax.all_gather(both, axis, axis=dim, tiled=True)  67.7 us
    all_to_all x1, blocking collectives, sum_at_owner(): lax.all_to_all(parts, axis, split_axis=0, concat_axis=0, tiled=True)  66.8 us
    all_to_all x1, waiting for transfers between devices, from_everyone(): return lax.all_to_all(copies, axis, split_axis=0, concat_axis=0, tiled=True)  56.3 us
    all_to_all x1, waiting for transfers between devices, supernode_pass(): lax.all_to_all(grouped, 'row', split_axis=0, concat_axis=1, tiled=True)  16 us
    all_to_all x1, blocking collectives, supernode_pass(): lax.all_to_all(held[None], 'col', split_axis=3, concat_axis=0, tiled=True)  15.7 us
  transfers between devices with their start and end apart: 3, of which 3 were waited for; matrix products, arithmetic and copies ran while one was open for 1% of the time, Pallas kernels for 0%

commit v1 on v0

--- a/solution.py
+++ b/solution.py
@@ -46,7 +46,10 @@
     local_rows = held.shape[0]
     nodes = held.shape[1]
     narrow = held.shape[2] // count_col
-    by_column = lax.all_to_all(held[None], "col", split_axis=3, concat_axis=0, tiled=True)
+    by_column = jnp.concatenate(
+        lax.all_to_all(jnp.stack(jnp.split(held[None], lax.axis_size("col"), axis=3)), "col", 0, 0),
+        axis=0,
+    )
     grouped = by_column.reshape(count_row, 1, ratio, local_rows, nodes, narrow)
     moved = lax.all_to_all(grouped, "row", split_axis=0, concat_axis=1, tiled=True)
     ordered = jnp.transpose(moved[0], (1, 0, 2, 3, 4)).reshape(

time: 267 us -> 266 us (level)
    unnamed x11 -> x42, local copies, waits for them, and re-layouts: 5.09 us -> 6.1 us
where the time goes in v1:
time: 266 us
  waiting for transfers between devices  140 us (53%)
  blocking collectives  82.6 us (31%)
  between operations  14.2 us (5%)
  local copies, waits for them, and re-layouts  10.1 us (4%)
  starting transfers between devices  7.2 us (3%)
  other arithmetic  6.96 us (3%)
  matrix products  4.68 us (2%)
    all_gather x1, waiting for transfers between devices, in_one_piece(): lax.all_gather(both, axis, axis=dim, tiled=True)  67.7 us
    all_to_all x1, blocking collectives, sum_at_owner(): lax.all_to_all(parts, axis, split_axis=0, concat_axis=0, tiled=True)  66.9 us
    all_to_all x1, waiting for transfers between devices, from_everyone(): return lax.all_to_all(copies, axis, split_axis=0, concat_axis=0, tiled=True)  56.3 us
    all_to_all x1, waiting for transfers between devices, supernode_pass(): lax.all_to_all(grouped, 'row', split_axis=0, concat_axis=1, tiled=True)  16 us
    all_to_all x1, blocking collectives, supernode_pass(): lax.all_to_all(jnp.stack(jnp.split(held[None], lax.axis_size('col'), axis...  15.7 us
    unnamed x42, local copies, waits for them, and re-layouts  6.1 us
  transfers between devices with their start and end apart: 3, of which 3 were waited for; matrix products, arithmetic and copies ran while one was open for 1% of the time, Pallas kernels for 0%

profile of v1, /device:TPU:32, one launch (start us, length us, event | category | flops | bytes accessed | tf_op | source)
XLA Modules:
  0.0 265.7 jit_solution(16776627218916270705)
XLA Ops:
  7.2 0.7 fusion.8
  8.0 0.9 copy_multiply_fusion
  8.9 0.6 pad_maximum_fusion
  9.6 1.2 copy.94
  10.8 0.7 convert_element_type.6
  11.7 67.7 %all-gather.2.cloned.1.call-done = f32[512,2,513]{2,0,1:T(8,128)} async-done(((f32[16,2,513]{2,0,1:T(8,128)}), f32[512,2,513]{2,0,1:T(8,128)}) %all-gather.2.cloned.1.call-update) | async-done | bytes 2101264 | tf_op jit(solution)/shard_map/all_gather | solution.py:10
  79.4 3.5 %fusion.2 = f32[256,2,512]{2,0,1:T(8,128)S(1)} fusion(f32[512,2,513]{2,0,1:T(8,128)} %all-gather.2.cloned.1.call-done, f32[512,256]{0,1:T(8,128)S(1)} %bitcast_multiply_fusion), kind=kOutput, calls=%fused_computation.2 | convolution fusion | flops 1610612736 | bytes 3670016 | tf_op jit(solution)/shard_map/ij,ika->jka/dot_general | solution.py:42
  83.0 66.9 %all_to_all.24 = f32[16,16,2,512]{3,1,2,0:T(8,128)} all-to-all(f32[16,16,2,512]{3,1,2,0:T(8,128)S(1)} %copy.97), channel_id=1, replica_groups=mesh['row'=16,'col'=32] {'row'}, dimensions={0} | all-to-all | bytes 2097152 | tf_op jit(solution)/shard_map/all_to_all | solution.py:25
  149.9 1.4 reduce_sum.18
  153.7 15.7 %all_to_all.25 = f32[32,1,512]{2,1,0:T(1,128)S(1)} all-to-all(f32[32,1,512]{2,1,0:T(1,128)S(1)} %reshape.32), channel_id=1, replica_groups=mesh['row'=16,'col'=32] {'col'}, dimensions={0} | all-to-all | bytes 131072 | tf_op jit(solution)/shard_map/all_to_all | solution.py:50
  169.4 0.5 broadcast.3
  169.9 0.8 reduce.2
  170.9 0.9 reshape.34
  171.8 3.5 %all-to-all-start.2 = ((f32[16,1,1024]{2,1,0:T(1,128)}), f32[16,1,1024]{2,1,0:T(1,128)S(1)}, u32[]{:S(2)}, u32[]{:S(2)}) async-start(f32[16,1,1024]{2,1,0:T(1,128)} %reshape.34), calls=%async_computation.2 | async-start | bytes 131072 | tf_op jit(solution)/shard_map/all_to_all | solution.py:54
  175.5 16.0 %all-to-all-done.2 = f32[16,1,1024]{2,1,0:T(1,128)S(1)} async-done(((f32[16,1,1024]{2,1,0:T(1,128)}), f32[16,1,1024]{2,1,0:T(1,128)S(1)}, u32[]{:S(2)}, u32[]{:S(2)}) %all-to-all-start.2) | async-done | bytes 65568 | tf_op jit(solution)/shard_map/all_to_all | solution.py:54
  191.5 0.8 reduce.3
  192.6 0.8 negate_bitcast_fusion
  193.4 1.5 copy.99
  195.2 1.2 fusion.4
  196.4 1.1 broadcast_in_dim.20
  197.5 3.7 %all-to-all-start.3 = ((f32[16,16,2,512]{3,1,2,0:T(8,128)}), f32[16,16,2,512]{3,1,2,0:T(8,128)S(1)}, u32[]{:S(2)}, u32[]{:S(2)}) async-start(f32[16,16,2,512]{3,1,2,0:T(8,128)} %broadcast_in_dim.20), calls=%async_computation.3 | async-start | bytes 2097152 | tf_op jit(solution)/shard_map/all_to_all | solution.py:31
  201.2 0.7 copy.101
  201.8 56.3 %all-to-all-done.3 = f32[16,16,2,512]{3,1,2,0:T(8,128)S(1)} async-done(((f32[16,16,2,512]{3,1,2,0:T(8,128)}), f32[16,16,2,512]{3,1,2,0:T(8,128)S(1)}, u32[]{:S(2)}, u32[]{:S(2)}) %all-to-all-start.3) | async-done | bytes 1048608 | tf_op jit(solution)/shard_map/all_to_all | solution.py:31
  258.2 0.7 copy.102
  (51 shorter events, 3.7 us)
Async XLA Ops:
  7.2 72.3 %all-gather.2.cloned.1.call-start = ((), (), s32[]{:S(2)}) async-start(), calls=%async_computation.4 | async-start | bytes 2703360 | tf_op jit(solution)/shard_map/all_gather | solution.py:10
  149.9 25.4 %copy-start = (f32[512,2,513]{2,0,1:T(8,128)S(1)}, f32[512,2,513]{2,0,1:T(8,128)}, u32[]{:S(2)}) copy-start(f32[512,2,513]{2,0,1:T(8,128)} %all-gather.2.cloned.1.call-done) | copy-start | bytes 6303748
  171.8 19.8 %all-to-all-start.2 = ((f32[16,1,1024]{2,1,0:T(1,128)}), f32[16,1,1024]{2,1,0:T(1,128)S(1)}, u32[]{:S(2)}, u32[]{:S(2)}) async-start(f32[16,1,1024]{2,1,0:T(1,128)} %reshape.34), calls=%async_computation.2 | async-start | bytes 131072 | tf_op jit(solution)/shard_map/all_to_all | solution.py:54
  196.4 61.8 %copy-start.1 = (f32[16,2,512]{2,1,0:T(2,128)S(1)}, f32[16,2,512]{2,1,0:T(2,128)}, u32[]{:S(2)}) copy-start(f32[16,2,512]{2,1,0:T(2,128)} %param.9) | copy-start | bytes 196612
  197.5 60.6 %all-to-all-start.3 = ((f32[16,16,2,512]{3,1,2,0:T(8,128)}), f32[16,16,2,512]{3,1,2,0:T(8,128)S(1)}, u32[]{:S(2)}, u32[]{:S(2)}) async-start(f32[16,16,2,512]{3,1,2,0:T(8,128)} %broadcast_in_dim.20), calls=%async_computation.3 | async-start | bytes 2097152 | tf_op jit(solution)/shard_map/all_to_all | solution.py:31
Sparse Core Ops, SparseCore 0:
  10.1 69.3 all-gather.1
